TPU v7x, 256 devices: a whole 4x4x8 slice. The times are simulated.
256 devices in a mesh: dp: 4 (over y), tensor: 16 (over z, core), owner: 4 (over x).
Axes of the slice: x: 4, y: 4, z: 8, core: 2. Of those that a mesh axis runs over, the one named last changes fastest.
Arguments:
- queries: bfloat16 [512, 8192], P(('dp', 'tensor'), 'owner'), may hold values from -360 to 360
- cached_key_rows: bfloat16 [512, 512, 8, 128], P(('dp', 'tensor'), None, 'owner'), may hold values from -6 to 6
- cached_value_rows: bfloat16 [512, 512, 8, 128], P(('dp', 'tensor'), None, 'owner'), may hold values from -6 to 6
- newest_key: bfloat16 [512, 8, 128], P(('dp', 'tensor'), 'owner'), may hold values from -6 to 6
- newest_value: bfloat16 [512, 8, 128], P(('dp', 'tensor'), 'owner'), may hold values from -6 to 6
- output_weight: bfloat16 [8, 1024, 8192], P('owner', 'tensor'), may hold values from -0.75 to 0.75
- adapter_down_weight: bfloat16 [128, 8, 1024, 64], P('owner', None, 'tensor'), may hold values from -0.5 to 0.5
- adapter_up_weight: bfloat16 [128, 64, 8192], P('owner', None, 'tensor'), may hold values from -0.75 to 0.75
- adapter_store_row: int32 [128], replicated, may hold values from 0 to 127, each once
- adapters_by_group: int32 [4, 16], P('dp'), may hold values from 0 to 127, as said below
- adapter_per_row: int32 [512], P('dp'), may hold values from 0 to 127, as said below
Outputs:
- output: bfloat16 [512, 8192], P('dp', ('tensor', 'owner'))
Inputs may be any that keep to these rules, and one draw needn't show every extreme that they name: `adapter_per_row`: the rows g * 128 to (g + 1) * 128 - 1 form dp group g; each row's adapter is one of its group's listed adapters, and each listed one is used by some row of the group. `adapters_by_group`: the 16 adapters of a group are distinct.
All inputs are finite; a program needn't handle non-finite values.
Results may differ from a plain program's by a relative error of at most 0.015.
Values may be sent and summed in bfloat16 or wider, within the bound.
No kernel may reach another device: no remote copies, remote signals or barrier semaphores. Data moves between devices by JAX's collectives and lax.ppermute only.
A program may use at most 128 MiB of HBM per device.

v0:
```python
import jax
import jax.numpy as jnp
from jax import lax
from jax.sharding import PartitionSpec as P

ADAPTER_SCALE = 2.0


def shards(
    queries,
    cached_key_rows,
    cached_value_rows,
    newest_key,
    newest_value,
    output_weight,
    adapter_down_weight,
    adapter_up_weight,
    adapter_store_row,
    adapters_by_group,
    adapter_per_row,
):
    owner_index = lax.axis_index("owner")
    row_count = queries.shape[0]
    local_heads = newest_key.shape[1]
    head_width = newest_key.shape[2]
    group_width = queries.shape[1] // local_heads
    query_heads = queries.reshape(row_count, local_heads, group_width // head_width, head_width)
    inverse_root = head_width ** (-0.5)
    scores = (
        jnp.einsum(
            "rkgh,rckh->rkgc", query_heads, cached_key_rows, preferred_element_type=jnp.float32
        )
        * inverse_root
    )
    fresh_score = (
        jnp.einsum("rkgh,rkh->rkg", query_heads, newest_key, preferred_element_type=jnp.float32)
        * inverse_root
    )
    overall = jnp.maximum(jnp.max(scores, axis=-1), fresh_score)
    weights_exp = jnp.exp(scores - overall[..., None])
    fresh_weight = jnp.exp(fresh_score - overall)
    denominator = jnp.sum(weights_exp, axis=-1) + fresh_weight
    mixed = jnp.einsum(
        "rkgc,rckh->rkgh", weights_exp, cached_value_rows, preferred_element_type=jnp.float32
    )
    mixed = mixed + fresh_weight[..., None] * newest_value.astype(jnp.float32)[:, :, None, :]
    mixed = (
        (mixed / denominator[..., None])
        .astype(jnp.bfloat16)
        .reshape(row_count, local_heads, group_width)
    )
    attention = lax.all_to_all(mixed, "tensor", split_axis=2, concat_axis=0, tiled=True)
    slot_ids = adapters_by_group[0]
    adapter_total = adapter_store_row.shape[0]
    matches = slot_ids[:, None] == jnp.arange(adapter_total, dtype=jnp.int32)[None, :]
    slot_home = jnp.sum(jnp.where(matches, adapter_store_row[None, :], 0), axis=1)
    store_count = adapter_down_weight.shape[0]
    slot_match = (adapter_per_row[:, None] == slot_ids[None, :]).astype(jnp.float32)
    position = slot_home - owner_index * store_count
    is_present = (position >= 0) & (position < store_count)
    clamped_index = jnp.clip(position, 0, store_count - 1)
    down_projected = jnp.where(
        is_present[:, None, None, None], adapter_down_weight[clamped_index], 0
    )
    up_projected = jnp.where(is_present[:, None, None], adapter_up_weight[clamped_index], 0)
    down_total, up_total = (
        lax.psum_scatter(down_projected, "owner", scatter_dimension=1, tiled=True).astype(
            jnp.float32
        ),
        lax.psum_scatter(up_projected, "owner", scatter_dimension=2, tiled=True).astype(
            jnp.float32
        ),
    )
    slot_down = down_total.astype(jnp.bfloat16)
    slot_up = up_total.astype(jnp.bfloat16)
    rank_slots = jnp.einsum(
        "rkf,skfn->rsn", attention, slot_down, preferred_element_type=jnp.float32
    )
    rank_part = jnp.sum(slot_match[:, :, None] * rank_slots, axis=1)
    rank_code = lax.psum(rank_part, ("tensor", "owner")).astype(jnp.bfloat16)
    update_slots = jnp.einsum("rn,snc->rsc", rank_code, slot_up, preferred_element_type=jnp.float32)
    adapter_delta = jnp.sum(slot_match[:, :, None] * update_slots, axis=1)
    partial_sum = jnp.einsum(
        "rkf,kfd->rd", attention, output_weight, preferred_element_type=jnp.float32
    )
    base_output = lax.psum_scatter(
        partial_sum, ("tensor", "owner"), scatter_dimension=1, tiled=True
    )
    return (base_output + ADAPTER_SCALE * adapter_delta).astype(jnp.bfloat16)


def solution(mesh):
    return jax.shard_map(
        shards,
        mesh=mesh,
        in_specs=(
            P(("dp", "tensor"), "owner"),
            P(("dp", "tensor"), None, "owner", None),
            P(("dp", "tensor"), None, "owner", None),
            P(("dp", "tensor"), "owner", None),
            P(("dp", "tensor"), "owner", None),
            P("owner", "tensor", None),
            P("owner", None, "tensor", None),
            P("owner", None, "tensor"),
            P(),
            P("dp", None),
            P("dp"),
        ),
        out_specs=P("dp", ("tensor", "owner")),
        check_vma=False,
    )
```

profile of v0, /device:TPU:8, one launch (start us, length us, event | category | flops | bytes accessed | tf_op | source)
XLA Modules:
  0.0 342.8 jit_solution(8786427746575031881)
XLA Ops:
  6.5 0.0 copy-start
  6.5 0.0 all-reduce.3.cloned.1.call-start
  6.5 1.0 select_reduce_fusion
  7.6 4.3 %gather_fusion = bf16[16,8,64,64]{3,2,1,0:T(8,128)(2,1)} fusion(bf16[32,8,64,64]{3,2,1,0:T(8,128)(2,1)} %param.17, s32[1024]{0:T(1024)S(1)} %pad_clamp_fusion), kind=kCustom, calls=%fused_computation | custom fusion | bytes 2097216 | tf_op jit(solution)/shard_map/gather | solution.py:63
  11.9 3.1 broadcast_select_fusion
  15.1 0.0 all-reduce.3.cloned.1.call-update
  15.1 0.0 reduce-scatter.8.cloned.1.call-start
  15.1 3.2 gather_fusion.1
  18.3 1.4 broadcast_select_fusion.1
  19.7 2.9 copy.60
  22.6 0.0 copy-start.2
  22.6 0.0 copy-start.1
  22.6 0.0 copy-start.6
  22.6 4.2 %reshape.104 = bf16[512,1024]{1,0:T(8,128)(2,1)} reshape(bf16[512,16,64]{2,1,0:T(8,128)(2,1)} %bitcast.44) | data formatting | bytes 2097152
  26.8 0.0 reduce-scatter.8.cloned.1.call-update
  26.8 0.0 reduce-scatter.6.cloned.1.call-start
  26.9 0.0 copy-done.2
  26.9 0.0 copy-start.5
  26.9 0.0 copy-done.1
  26.9 0.0 copy-done.6
  26.9 0.1 fusion.25
  27.0 2.4 fusion.34
  29.5 0.2 fusion.21
  29.7 0.0 copy-done.5
  29.8 0.5 fusion.16
  30.2 0.3 copy.54
  30.5 0.5 reshape.107
  31.1 16.3 %all_to_all.18 = bf16[16,2,512]{2,1,0:T(2,128)(2,1)S(1)} all-to-all(bf16[16,2,512]{2,1,0:T(2,128)(2,1)S(1)} %reshape.107), channel_id=1, replica_groups=mesh['dp'=4,'tensor'=16,'owner'=4] {'tensor'}, dimensions={0} | all-to-all | bytes 65536 | tf_op jit(solution)/shard_map/all_to_all | solution.py:52
  47.3 0.6 reshape.108
  48.0 0.4 copy.56
  48.4 0.0 copy-done
  48.4 2.7 convolution_bitcast_fusion
  51.0 0.0 copy-start.7
  51.0 0.0 copy-start.3
  51.0 0.0 copy-start.4
  51.1 0.0 reduce-scatter.6.cloned.1.call-update
  51.1 0.6 copy-done.7
  51.7 0.6 dynamic-slice
  53.0 0.0 copy-done.3
  53.0 0.0 copy-done.4
  53.0 0.1 compare_convert_fusion
  53.1 28.9 %all-reduce.3.cloned.1.call-done = bf16[16,8,64,64]{3,2,1,0:T(8,128)(2,1)} async-done(((bf16[16,8,64,64]{3,2,1,0:T(8,128)(2,1)}), bf16[16,8,64,64]{3,2,1,0:T(8,128)(2,1)}) %all-reduce.3.cloned.1.call-update) | async-done | bytes 1048592
  81.9 1.4 fusion.6
  83.3 249.7 %psum.7 = bf16[128,64]{0,1:T(8,128)(2,1)S(1)} all-reduce(f32[128,64]{0,1:T(8,128)S(1)} %fusion.6), channel_id=1, replica_groups=mesh['dp'=4,'tensor'=16,'owner'=4] {'tensor','owner'}, use_global_device_ids=true, to_apply=%region_6.7 | all-reduce | flops 8192 | bytes 49152 | tf_op jit(solution)/shard_map/psum | solution.py:80
  333.0 1.3 reshape.105
  334.4 0.4 fusion.4
  334.8 0.0 reduce-scatter.6.cloned.1.call-done
  334.8 1.5 add_convert_fusion
  (7 shorter events, 0.1 us)
Async XLA Ops:
  6.5 41.8 %copy-start = (bf16[2,64,8192]{2,1,0:T(8,128)(2,1)S(1)}, bf16[2,64,8192]{2,1,0:T(8,128)(2,1)}, u32[]{:S(2)}) copy-start(bf16[2,64,8192]{2,1,0:T(8,128)(2,1)} %param.16) | copy-start | bytes 6291460
  6.5 75.4 %all-reduce.3.cloned.1.call-start = ((), (), s32[]{:S(2)}) async-start(), calls=%async_computation.5 | async-start | bytes 4194304
  15.1 317.9 %reduce-scatter.8.cloned.1.call-start = ((), (), s32[]{:S(2)}) async-start(), calls=%async_computation.4 | async-start | bytes 1310720
  22.6 4.2 %copy-start.2 = (bf16[8,2,128]{2,1,0:T(2,128)(2,1)S(1)}, bf16[8,2,128]{2,1,0:T(2,128)(2,1)}, u32[]{:S(2)}) copy-start(bf16[8,2,128]{2,1,0:T(2,128)(2,1)} %param.15) | copy-start | bytes 12292
  22.6 4.3 %copy-start.1 = (bf16[8,2048]{1,0:T(8,128)(2,1)S(1)}, bf16[8,2048]{1,0:T(8,128)(2,1)}, u32[]{:S(2)}) copy-start(bf16[8,2048]{1,0:T(8,128)(2,1)} %param.11) | copy-start | bytes 98308
  22.6 4.3 %copy-start.6 = (bf16[8,2,128]{2,1,0:T(2,128)(2,1)S(1)}, bf16[8,2,128]{2,1,0:T(2,128)(2,1)}, u32[]{:S(2)}) copy-start(bf16[8,2,128]{2,1,0:T(2,128)(2,1)} %param.14) | copy-start | bytes 12292
  26.8 308.0 %reduce-scatter.6.cloned.1.call-start = ((), (), s32[]{:S(2)}) async-start(), calls=%async_computation.3 | async-start | bytes 4259840 | tf_op jit(solution)/shard_map/reduce_scatter | solution.py:86
  26.9 2.9 copy-start.5
  51.0 0.7 copy-start.7
  51.0 1.9 copy-start.3
  51.0 1.9 copy-start.4
Sparse Core Ops, SparseCore 0:
  15.2 66.6 all-reduce.2
  84.6 25.9 reduce-scatter.7
  114.8 143.6 reduce-scatter.5
where the time goes:
time: 343 us
  blocking collectives  266 us (78%)
  waiting for transfers between devices  28.9 us (8%)
  local copies, waits for them, and re-layouts  19 us (6%)
  between operations  13.9 us (4%)
  matrix products  7.54 us (2%)
  other arithmetic  7.3 us (2%)
    psum x1, blocking collectives, shards(): rank_code = lax.psum(rank_part, ('tensor', 'owner')).astype(jnp.bfloat16)  250 us
    unnamed x5, waiting for transfers between devices  28.9 us
    all_to_all x1, blocking collectives, shards(): lax.all_to_all(mixed, 'tensor', split_axis=2, concat_axis=0, tiled=True)  16.3 us
    unnamed x22, local copies, waits for them, and re-layouts  10.8 us
  transfers between devices with their start and end apart: 3, of which 1 were waited for; matrix products, arithmetic and copies ran while one was open for 7% of the time, Pallas kernels for 0%

commit v1 on v0

--- a/solution.py
+++ b/solution.py
@@ -77,7 +77,7 @@
         "rkf,skfn->rsn", attention, slot_down, preferred_element_type=jnp.float32
     )
     rank_part = jnp.sum(slot_match[:, :, None] * rank_slots, axis=1)
-    rank_code = lax.psum(rank_part, ("tensor", "owner")).astype(jnp.bfloat16)
+    rank_code = lax.psum(lax.psum(rank_part, "owner"), "tensor").astype(jnp.bfloat16)
     update_slots = jnp.einsum("rn,snc->rsc", rank_code, slot_up, preferred_element_type=jnp.float32)
     adapter_delta = jnp.sum(slot_match[:, :, None] * update_slots, axis=1)
     partial_sum = jnp.einsum(

time: 343 us -> 267 us (0.78)
  blocking collectives: 266 us -> 77.7 us
  waiting for transfers between devices: 28.9 us -> 141 us
    psum x1 -> x2, blocking collectives: 250 us -> 61.4 us  [the longest x1 46.2 us: shards(): lax.psum(lax.psum(rank_part, 'owner'), 'tensor').astype(jnp.bfloat16)]
    reduce_scatter x1, waiting for transfers between devices: 0.02 us -> 112 us  [shards(): lax.psum_scatter(partial_sum, ('tensor', 'owner'), scatter_dimension=1, t...]
  transfers between devices with their start and end apart: 3 -> 3, of which waited for: 1 -> 2; matrix products, arithmetic and copies ran while one was open for 7% -> 9% of each run, Pallas kernels for 0% -> 0%
where the time goes in v1:
time: 267 us; the launch traced here: 266 us
  waiting for transfers between devices  141 us (53%)
  blocking collectives  77.7 us (29%)
  local copies, waits for them, and re-layouts  19 us (7%)
  between operations  13.9 us (5%)
  matrix products  7.54 us (3%)
  other arithmetic  7.3 us (3%)
    reduce_scatter x1, waiting for transfers between devices, shards(): lax.psum_scatter(partial_sum, ('tensor', 'owner'), scatter_dimension=1, t...  112 us
    psum x1, blocking collectives, shards(): lax.psum(lax.psum(rank_part, 'owner'), 'tensor').astype(jnp.bfloat16)  46.2 us
    unnamed x5, waiting for transfers between devices  28.9 us
    all_to_all x1, blocking collectives, shards(): lax.all_to_all(mixed, 'tensor', split_axis=2, concat_axis=0, tiled=True)  16.3 us
    psum x1, blocking collectives, shards(): lax.psum(rank_part, 'owner')  15.2 us
    unnamed x22, local copies, waits for them, and re-layouts  10.8 us
  transfers between devices with their start and end apart: 3, of which 2 were waited for; matrix products, arithmetic and copies ran while one was open for 9% of the time, Pallas kernels for 0%

profile of v1, /device:TPU:8, one launch (start us, length us, event | category | flops | bytes accessed | tf_op | source)
XLA Modules:
  0.0 266.4 jit_solution(1649633559219911371)
XLA Ops:
  6.5 0.0 copy-start
  6.5 0.0 all-reduce.3.cloned.1.call-start
  6.5 1.0 select_reduce_fusion
  7.6 4.3 %gather_fusion = bf16[16,8,64,64]{3,2,1,0:T(8,128)(2,1)} fusion(bf16[32,8,64,64]{3,2,1,0:T(8,128)(2,1)} %param.17, s32[1024]{0:T(1024)S(1)} %pad_clamp_fusion), kind=kCustom, calls=%fused_computation | custom fusion | bytes 2097216 | tf_op jit(solution)/shard_map/gather | solution.py:63
  11.9 3.1 %broadcast_select_fusion = bf16[16,8,64,64]{3,2,1,0:T(8,128)(2,1)} fusion(bf16[16,8,64,64]{3,2,1,0:T(8,128)(2,1)} %gather_fusion, pred[16]{0:T(512)(128)(4,1)S(1)} %compare_and_fusion), kind=kLoop, calls=%fused_computation.7 | loop fusion | flops 524288 | bytes 2097168 | tf_op jit(solution)/shard_map/jit(_where)/select_n | solution.py:62
  15.1 0.0 all-reduce.3.cloned.1.call-update
  15.1 0.0 reduce-scatter.8.cloned.1.call-start
  15.1 3.2 %gather_fusion.1 = bf16[16,64,512]{2,1,0:T(8,128)(2,1)} fusion(bf16[32,64,512]{2,1,0:T(8,128)(2,1)} %param.18, s32[1024]{0:T(1024)S(1)} %pad_clamp_fusion), kind=kCustom, calls=%fused_computation.1 | custom fusion | bytes 2097216 | tf_op jit(solution)/shard_map/gather | solution.py:65
  18.3 1.4 broadcast_select_fusion.1
  19.7 2.9 %copy.60 = bf16[16,64,512]{1,0,2:T(8,128)(2,1)} copy(bf16[16,64,512]{2,1,0:T(8,128)(2,1)S(1)} %broadcast_select_fusion.1) | data formatting | bytes 2097152
  22.6 0.0 copy-start.2
  22.6 0.0 copy-start.1
  22.6 0.0 copy-start.6
  22.6 4.2 %reshape.104 = bf16[512,1024]{1,0:T(8,128)(2,1)} reshape(bf16[512,16,64]{2,1,0:T(8,128)(2,1)} %bitcast.44) | data formatting | bytes 2097152
  26.8 0.0 reduce-scatter.8.cloned.1.call-update
  26.8 0.0 reduce-scatter.6.cloned.1.call-start
  26.9 0.0 copy-done.2
  26.9 0.0 copy-start.5
  26.9 0.0 copy-done.1
  26.9 0.0 copy-done.6
  26.9 0.1 fusion.25
  27.0 2.4 fusion.34
  29.5 0.2 fusion.21
  29.7 0.0 copy-done.5
  29.8 0.5 fusion.16
  30.2 0.3 copy.54
  30.5 0.5 reshape.107
  31.1 16.3 %all_to_all.18 = bf16[16,2,512]{2,1,0:T(2,128)(2,1)S(1)} all-to-all(bf16[16,2,512]{2,1,0:T(2,128)(2,1)S(1)} %reshape.107), channel_id=1, replica_groups=mesh['dp'=4,'tensor'=16,'owner'=4] {'tensor'}, dimensions={0} | all-to-all | bytes 65536 | tf_op jit(solution)/shard_map/all_to_all | solution.py:52
  47.3 0.6 reshape.108
  48.0 0.4 copy.56
  48.4 0.0 copy-done
  48.4 2.7 %convolution_bitcast_fusion = f32[128,8192]{1,0:T(8,128)} fusion(bf16[2,64,8192]{2,1,0:T(8,128)(2,1)S(1)} %copy-done, bf16[8,2,16,64]{3,0,2,1:T(8,128)(2,1)S(1)} %copy.56), kind=kOutput, calls=%fused_computation.2 | convolution fusion | flops 268435456 | bytes 6324224 | tf_op jit(solution)/shard_map/rkf,kfd->rd/dot_general | solution.py:83
  51.0 0.0 copy-start.7
  51.0 0.0 copy-start.3
  51.1 0.0 reduce-scatter.6.cloned.1.call-update
  51.1 0.6 copy-done.7
  51.7 0.6 dynamic-slice
  53.0 0.0 copy-done.3
  53.0 0.0 copy-done.4
  53.0 0.1 compare_convert_fusion
  53.1 28.9 %all-reduce.3.cloned.1.call-done = bf16[16,8,64,64]{3,2,1,0:T(8,128)(2,1)} async-done(((bf16[16,8,64,64]{3,2,1,0:T(8,128)(2,1)}), bf16[16,8,64,64]{3,2,1,0:T(8,128)(2,1)}) %all-reduce.3.cloned.1.call-update) | async-done | bytes 1048592
  81.9 1.4 fusion.6
  83.3 15.2 %psum.14 = f32[128,64]{0,1:T(8,128)S(1)} all-reduce(f32[128,64]{0,1:T(8,128)S(1)} %fusion.6), channel_id=1, replica_groups=mesh['dp'=4,'tensor'=16,'owner'=4] {'owner'}, use_global_device_ids=true, to_apply=%region_6.7 | all-reduce | flops 8192 | bytes 65536 | tf_op jit(solution)/shard_map/psum | solution.py:80
  98.5 46.2 %psum.15 = bf16[128,64]{0,1:T(8,128)(2,1)S(1)} all-reduce(f32[128,64]{0,1:T(8,128)S(1)} %psum.14), channel_id=1, replica_groups=mesh['dp'=4,'tensor'=16,'owner'=4] {'tensor'}, use_global_device_ids=true, to_apply=%region_7.8 | all-reduce | flops 8192 | bytes 49152 | tf_op jit(solution)/shard_map/psum | solution.py:80
  144.8 1.3 reshape.105
  146.1 0.4 fusion.4
  146.5 111.8 %reduce-scatter.6.cloned.1.call-done = f32[128,128]{1,0:T(8,128)} async-done(((f32[128,8192]{1,0:T(8,128)}), f32[128,128]{1,0:T(8,128)}) %reduce-scatter.6.cloned.1.call-update) | async-done | bytes 65552 | tf_op jit(solution)/shard_map/reduce_scatter | solution.py:86
  258.4 1.5 add_convert_fusion
  (8 shorter events, 0.1 us)
Async XLA Ops:
  6.5 41.8 %copy-start = (bf16[2,64,8192]{2,1,0:T(8,128)(2,1)S(1)}, bf16[2,64,8192]{2,1,0:T(8,128)(2,1)}, u32[]{:S(2)}) copy-start(bf16[2,64,8192]{2,1,0:T(8,128)(2,1)} %param.16) | copy-start | bytes 6291460
  6.5 75.4 %all-reduce.3.cloned.1.call-start = ((), (), s32[]{:S(2)}) async-start(), calls=%async_computation.5 | async-start | bytes 4194304
  15.1 129.7 %reduce-scatter.8.cloned.1.call-start = ((), (), s32[]{:S(2)}) async-start(), calls=%async_computation.4 | async-start | bytes 1310720
  22.6 4.2 %copy-start.2 = (bf16[8,2,128]{2,1,0:T(2,128)(2,1)S(1)}, bf16[8,2,128]{2,1,0:T(2,128)(2,1)}, u32[]{:S(2)}) copy-start(bf16[8,2,128]{2,1,0:T(2,128)(2,1)} %param.15) | copy-start | bytes 12292
  22.6 4.3 %copy-start.1 = (bf16[8,2048]{1,0:T(8,128)(2,1)S(1)}, bf16[8,2048]{1,0:T(8,128)(2,1)}, u32[]{:S(2)}) copy-start(bf16[8,2048]{1,0:T(8,128)(2,1)} %param.11) | copy-start | bytes 98308
  22.6 4.3 %copy-start.6 = (bf16[8,2,128]{2,1,0:T(2,128)(2,1)S(1)}, bf16[8,2,128]{2,1,0:T(2,128)(2,1)}, u32[]{:S(2)}) copy-start(bf16[8,2,128]{2,1,0:T(2,128)(2,1)} %param.14) | copy-start | bytes 12292
  26.8 231.6 %reduce-scatter.6.cloned.1.call-start = ((), (), s32[]{:S(2)}) async-start(), calls=%async_computation.3 | async-start | bytes 4259840 | tf_op jit(solution)/shard_map/reduce_scatter | solution.py:86
  26.9 2.9 %copy-start.5 = (bf16[8,512,2,128]{3,2,1,0:T(2,128)(2,1)S(1)}, bf16[8,512,2,128]{3,2,1,0:T(2,128)(2,1)}, u32[]{:S(2)}) copy-start(bf16[8,512,2,128]{3,2,1,0:T(2,128)(2,1)} %param.13) | copy-start | bytes 6291460
  51.0 0.7 copy-start.7
  51.0 1.9 copy-start.3
  51.0 1.9 copy-start.4
Sparse Core Ops, SparseCore 0:
  15.2 66.6 all-reduce.2
  84.6 25.8 reduce-scatter.7
  114.7 143.6 reduce-scatter.5
